TPU v7x, 256 devices: a whole 4x4x8 slice. The times are simulated.
256 devices in a mesh: wafer: 4 (over y), span: 64 (over z, x, core).
Axes of the slice: x: 4, y: 4, z: 8, core: 2. Of those that a mesh axis runs over, the one named last changes fastest.
Arguments:
- timestream: float32 [1536, 16384], P(('wafer', 'span')), may hold values from -6 to 6
- templates: float32 [64, 16384], P(None, 'span'), may hold values from -0.046875 to 0.046875
- bias_group: int32 [1536], P('wafer'), may hold values from 0 to 11, as said below
- det_weight: float32 [1536], P('wafer'), may hold values from 0.2 to 5
- cut_start: int32 [1536], P('wafer'), may hold values from 0 to 16383
- cut_len: int32 [1536], P('wafer'), may hold values from 1 to 511
- pointing: int32 [1536, 16384], P('wafer', 'span'), may hold values from 0 to 32767
- hit_tiles: int32 [64, 64], replicated, may hold values from 0 to 511, as said below
Outputs:
- fit_coeffs: float32 [1536, 64], P(('wafer', 'span'))
- rhs_map: float32 [512, 512], P('span', 'wafer')
- weight_map: float32 [512, 512], P('span', 'wafer')
Inputs may be any that keep to these rules, and one draw needn't show every extreme that they name: `bias_group`: within each wafer's 384 detectors every bias line holds exactly 32 detectors. `hit_tiles`: each row lists distinct tiles; tile t is owned by index t // 8 of span; every row holds exactly 2 tiles of each owner it names: of one owner common to all rows, and of 31 other owners.
All inputs are finite; a program needn't handle non-finite values.
Results may differ from a plain program's by a relative error of at most 0.0041.
Values sent between devices are 32-bit elements; how exact they have to be, the bound alone decides.
No kernel may reach another device: no remote copies, remote signals or barrier semaphores. Data moves between devices by JAX's collectives and lax.ppermute only.
A program may use at most 64 MiB of HBM per device.

v0:
```python
import math
import jax
import jax.numpy as jnp
from jax import lax
from jax.sharding import PartitionSpec as P

NGROUP = 12
TILE = 512
TILE_OWN = 8


def solve_normal(matrix, right_side):
    factor = jnp.linalg.cholesky(matrix)
    middle = lax.linalg.triangular_solve(factor, right_side, left_side=True, lower=True)
    return lax.linalg.triangular_solve(factor, middle, left_side=True, lower=True, transpose_a=True)


def bin_samples(weighted, sample_weight, pointing, tiles_listed):
    rows = weighted.shape[0]
    block_dets = math.gcd(rows, 64)
    block_count = rows // block_dets
    fine_width = min(128, TILE)
    coarse_width = tiles_listed * TILE // fine_width
    blocks = (
        weighted.reshape(block_count, -1),
        sample_weight.reshape(block_count, -1),
        pointing.reshape(block_count, -1),
    )
    zero_value = jnp.zeros((), jnp.bfloat16)

    def accumulate(totals, block_data):
        values_block, weights_block, points_block = block_data
        coarse_index = points_block // fine_width
        fine_index = points_block % fine_width
        coarse_hot = coarse_index[None, :] == jnp.arange(coarse_width, dtype=jnp.int32)[:, None]
        left_hot = jnp.concatenate(
            [
                jnp.where(coarse_hot, values_block[None, :], zero_value),
                jnp.where(coarse_hot, weights_block[None, :], zero_value),
            ],
            axis=0,
        )
        right_hot = (
            fine_index[None, :] == jnp.arange(fine_width, dtype=jnp.int32)[:, None]
        ).astype(jnp.bfloat16)
        product = lax.dot_general(
            left_hot, right_hot, (((1,), (1,)), ((), ())), preferred_element_type=jnp.float32
        )
        return (totals + product, None)

    totals, unused = lax.scan(
        accumulate, jnp.zeros((2 * coarse_width, fine_width), jnp.float32), blocks
    )
    return totals.reshape(2, tiles_listed, TILE)


def body(timestream, templates, bias_group, det_weight, cut_start, cut_len, pointing, hit_tiles):
    highest = lax.Precision.HIGHEST
    spans = lax.axis_size("span")
    own_index = lax.axis_index("span")
    det_dev = timestream.shape[0]
    span_len = templates.shape[1]
    det_wafer = det_dev * spans
    line_scale = NGROUP / det_wafer
    groups = lax.dynamic_slice_in_dim(bias_group, own_index * det_dev, det_dev)
    onehot = (groups[None, :] == jnp.arange(NGROUP, dtype=jnp.int32)[:, None]).astype(jnp.float32)
    line_sums = lax.psum(
        jnp.dot(onehot, timestream, precision=highest, preferred_element_type=jnp.float32), "span"
    )
    cleaned = timestream - jnp.dot(
        onehot.T, line_sums * line_scale, precision=highest, preferred_element_type=jnp.float32
    )
    all_templates = lax.all_gather(templates, "span", axis=1, tiled=True)
    normal_matrix = jnp.dot(
        all_templates, all_templates.T, precision=highest, preferred_element_type=jnp.float32
    )
    projection = jnp.dot(
        all_templates, cleaned.T, precision=highest, preferred_element_type=jnp.float32
    )
    amplitudes = solve_normal(normal_matrix, projection)
    fit_coeffs = amplitudes.T
    outgoing = cleaned - jnp.dot(
        amplitudes.T, all_templates, precision=highest, preferred_element_type=jnp.float32
    )
    regrouped = lax.all_to_all(outgoing, "span", split_axis=1, concat_axis=0, tiled=True)
    sample_time = own_index * span_len + jnp.arange(span_len, dtype=jnp.int32)
    inside = (sample_time[None, :] >= cut_start[:, None]) & (
        sample_time[None, :] < (cut_start + cut_len)[:, None]
    )
    sample_weight = jnp.where(inside, jnp.float32(0.0), det_weight[:, None]).astype(jnp.bfloat16)
    weighted = (sample_weight.astype(jnp.float32) * regrouped).astype(jnp.bfloat16)
    tiles_listed = hit_tiles.shape[1]
    partial_value = bin_samples(weighted, sample_weight, pointing, tiles_listed)
    shared = lax.psum_scatter(partial_value, "wafer", scatter_dimension=2, tiled=True)
    own_tiles = lax.dynamic_index_in_dim(hit_tiles, own_index, 0, keepdims=False)
    selector = (
        own_tiles[None, :] == jnp.arange(lax.axis_size("span") * TILE_OWN, dtype=jnp.int32)[:, None]
    ).astype(jnp.float32)
    owned_tiles = lax.psum_scatter(
        jnp.einsum("rs,ksp->rkp", selector, shared, precision=highest),
        "span",
        scatter_dimension=0,
        tiled=True,
    )
    return (fit_coeffs, owned_tiles[:, 0, :], owned_tiles[:, 1, :])


def solution(mesh):
    in_specs = (
        P(("wafer", "span"), None),
        P(None, "span"),
        P("wafer"),
        P("wafer"),
        P("wafer"),
        P("wafer"),
        P("wafer", "span"),
        P(),
    )
    out_specs = (P(("wafer", "span"), None), P("span", "wafer"), P("span", "wafer"))
    return jax.shard_map(body, mesh=mesh, in_specs=in_specs, out_specs=out_specs, check_vma=False)
```

profile of v0, /device:TPU:8, one launch (start us, length us, event | category | flops | bytes accessed | tf_op | source)
XLA Modules:
  0.0 608.7 jit_solution(14513693516777914590)
XLA Ops:
  7.2 0.8 dynamic_slice.27
  8.0 2.6 fusion.23
  10.7 0.7 all-gather.2.cloned.1.call-update
  11.4 190.2 %all-reduce.2.cloned.1.call-done = f32[12,16384]{1,0:T(8,128)} async-done(((f32[12,16384]{1,0:T(8,128)}), f32[12,16384]{1,0:T(8,128)}) %all-reduce.2.cloned.1.call-update) | async-done | bytes 786448 | tf_op jit(solution)/shard_map/psum | solution.py:67
  201.5 1.9 convolution_subtract_fusion.1
  203.5 73.8 %all-gather.2.cloned.1.call-done = f32[64,16384]{1,0:T(8,128)} async-done(((f32[64,256]{1,0:T(8,128)}), f32[64,16384]{1,0:T(8,128)}) %all-gather.2.cloned.1.call-update) | async-done | bytes 4194320 | tf_op jit(solution)/shard_map/all_gather | solution.py:73
  277.3 6.9 %fusion.27 = f32[64,64]{1,0:T(8,128)S(1)} fusion(f32[64,16384]{1,0:T(8,128)} %all-gather.2.cloned.1.call-done), kind=kOutput, calls=%fused_computation.53 | convolution fusion | flops 805306368 | bytes 4210688 | tf_op jit(solution)/shard_map/dot_general | solution.py:74
  284.4 5.8 cholesky.16
  290.2 0.6 compare_reduce_fusion
  290.9 0.7 fusion.17
  291.6 4.9 custom-call.8
  296.4 5.1 fusion.28
  301.5 0.3 fusion.20
  301.8 0.2 fusion.18
  302.0 5.1 convolution_subtract_fusion
  307.1 8.5 %all-to-all-start = ((f32[6,64,256]{2,0,1:T(8,128)}), f32[6,64,256]{2,0,1:T(8,128)S(1)}, u32[]{:S(2)}, u32[]{:S(2)}) async-start(f32[6,64,256]{2,0,1:T(8,128)} %bitcast.6), calls=%async_computation | async-start | bytes 1048576 | tf_op jit(solution)/shard_map/all_to_all | solution.py:85
  315.6 0.2 reduce-scatter.3.cloned.1.call-start
  315.9 0.1 broadcast_in_dim.75
  316.2 0.1 broadcast_bitcast_fusion
  316.3 0.1 copy.18
  316.4 0.1 broadcast_bitcast_fusion.2
  316.5 0.2 copy.16
  316.8 0.1 broadcast_bitcast_fusion.1
  316.9 0.2 copy.17
  317.2 0.1 reshape.56
  317.3 16.0 %all-to-all-done = f32[6,64,256]{2,0,1:T(8,128)S(1)} async-done(((f32[6,64,256]{2,0,1:T(8,128)}), f32[6,64,256]{2,0,1:T(8,128)S(1)}, u32[]{:S(2)}, u32[]{:S(2)}) %all-to-all-start) | async-done | bytes 393248 | tf_op jit(solution)/shard_map/all_to_all | solution.py:85
  333.2 0.1 all_to_all.17
  333.4 0.2 multiply_convert_fusion
  333.5 112.1 %while.13 = (s32[]{:T(128)}, f32[512,128]{1,0:T(8,128)S(1)}, s32[6,16384]{1,0:T(8,128)S(1)}, bf16[6,16384]{1,0:T(8,128)(2,1)S(1)}, bf16[6,16384]{1,0:T(8,128)(2,1)S(1)}, /*index=5*/s32[]{:T(128)}, s32[]{:T(128)}) while((s32[]{:T(128)}, f32[512,128]{1,0:T(8,128)S(1)}, s32[6,16384]{1,0:T(8,128)S(1)}, bf16[6,16384]{1,0:T(8,128)(2,1)S(1)}, ...), condition=%wide.region_4.5_spmd.clone, body=%wide.region_3.4_spmd.clone.sunk | while | flops 2196176896 | bytes 34734180 | solution.py:51
  333.6 0.4 dynamic-slice_reduce_fusion.3
  334.0 0.3 and_select_fusion.4
  334.3 0.1 and_select_fusion.5
  334.4 9.2 %fusion.43 = (bf16[256,16384]{1,0:T(8,128)(2,1)}, bf16[256,16384]{1,0:T(8,128)(2,1)}) fusion(s32[16384]{0:T(1024)S(1)} %bitcast.51, bf16[16384]{0:T(1024)(128)(2,1)S(1)} %get-tuple-element.149, bf16[16384]{0:T(1024)(128)(2,1)S(1)} %get-tuple-element.150), kind=kLoop, calls=%fused_computation.6.clone.1 | loop fusion | flops 12582912 | bytes 16908288 | tf_op jit(solution)/shard_map/while/body/eval_jaxpr/jit(_where)/select_n | solution.py:38
  343.6 8.6 %fusion.44 = f32[512,128]{1,0:T(8,128)S(1)} fusion(s32[16384]{0:T(1024)S(1)} %bitcast.55, bf16[256,16384]{1,0:T(8,128)(2,1)} %get-tuple-element.151, bf16[256,16384]{1,0:T(8,128)(2,1)} %get-tuple-element.152, f32[512,128]{1,0:T(8,128)S(1)} %get-tuple-element.161, pred[]{:T(512)S(6)} %compare.24), kind=kOutput, calls=%fused_computation.9.clone.1 | convolution fusion | flops 2183266304 | bytes 17367040 | tf_op jit(solution)/shard_map/while/body/eval_jaxpr/dot_general | solution.py:46
  352.3 0.4 dynamic-slice_reduce_fusion.3
  352.6 0.3 and_select_fusion.4
  353.0 0.1 and_select_fusion.5
  353.1 9.2 %fusion.43 = (bf16[256,16384]{1,0:T(8,128)(2,1)}, bf16[256,16384]{1,0:T(8,128)(2,1)}) fusion(s32[16384]{0:T(1024)S(1)} %bitcast.51, bf16[16384]{0:T(1024)(128)(2,1)S(1)} %get-tuple-element.149, bf16[16384]{0:T(1024)(128)(2,1)S(1)} %get-tuple-element.150), kind=kLoop, calls=%fused_computation.6.clone.1 | loop fusion | flops 12582912 | bytes 16908288 | tf_op jit(solution)/shard_map/while/body/eval_jaxpr/jit(_where)/select_n | solution.py:38
  362.3 8.6 %fusion.44 = f32[512,128]{1,0:T(8,128)S(1)} fusion(s32[16384]{0:T(1024)S(1)} %bitcast.55, bf16[256,16384]{1,0:T(8,128)(2,1)} %get-tuple-element.151, bf16[256,16384]{1,0:T(8,128)(2,1)} %get-tuple-element.152, f32[512,128]{1,0:T(8,128)S(1)} %get-tuple-element.161, pred[]{:T(512)S(6)} %compare.24), kind=kOutput, calls=%fused_computation.9.clone.1 | convolution fusion | flops 2183266304 | bytes 17367040 | tf_op jit(solution)/shard_map/while/body/eval_jaxpr/dot_general | solution.py:46
  370.9 0.4 dynamic-slice_reduce_fusion.3
  371.3 0.3 and_select_fusion.4
  371.7 0.1 and_select_fusion.5
  371.8 9.2 %fusion.43 = (bf16[256,16384]{1,0:T(8,128)(2,1)}, bf16[256,16384]{1,0:T(8,128)(2,1)}) fusion(s32[16384]{0:T(1024)S(1)} %bitcast.51, bf16[16384]{0:T(1024)(128)(2,1)S(1)} %get-tuple-element.149, bf16[16384]{0:T(1024)(128)(2,1)S(1)} %get-tuple-element.150), kind=kLoop, calls=%fused_computation.6.clone.1 | loop fusion | flops 12582912 | bytes 16908288 | tf_op jit(solution)/shard_map/while/body/eval_jaxpr/jit(_where)/select_n | solution.py:38
  381.0 8.6 %fusion.44 = f32[512,128]{1,0:T(8,128)S(1)} fusion(s32[16384]{0:T(1024)S(1)} %bitcast.55, bf16[256,16384]{1,0:T(8,128)(2,1)} %get-tuple-element.151, bf16[256,16384]{1,0:T(8,128)(2,1)} %get-tuple-element.152, f32[512,128]{1,0:T(8,128)S(1)} %get-tuple-element.161, pred[]{:T(512)S(6)} %compare.24), kind=kOutput, calls=%fused_computation.9.clone.1 | convolution fusion | flops 2183266304 | bytes 17367040 | tf_op jit(solution)/shard_map/while/body/eval_jaxpr/dot_general | solution.py:46
  389.6 0.4 dynamic-slice_reduce_fusion.3
  390.0 0.3 and_select_fusion.4
  390.4 0.1 and_select_fusion.5
  390.5 9.2 %fusion.43 = (bf16[256,16384]{1,0:T(8,128)(2,1)}, bf16[256,16384]{1,0:T(8,128)(2,1)}) fusion(s32[16384]{0:T(1024)S(1)} %bitcast.51, bf16[16384]{0:T(1024)(128)(2,1)S(1)} %get-tuple-element.149, bf16[16384]{0:T(1024)(128)(2,1)S(1)} %get-tuple-element.150), kind=kLoop, calls=%fused_computation.6.clone.1 | loop fusion | flops 12582912 | bytes 16908288 | tf_op jit(solution)/shard_map/while/body/eval_jaxpr/jit(_where)/select_n | solution.py:38
  399.7 8.6 %fusion.44 = f32[512,128]{1,0:T(8,128)S(1)} fusion(s32[16384]{0:T(1024)S(1)} %bitcast.55, bf16[256,16384]{1,0:T(8,128)(2,1)} %get-tuple-element.151, bf16[256,16384]{1,0:T(8,128)(2,1)} %get-tuple-element.152, f32[512,128]{1,0:T(8,128)S(1)} %get-tuple-element.161, pred[]{:T(512)S(6)} %compare.24), kind=kOutput, calls=%fused_computation.9.clone.1 | convolution fusion | flops 2183266304 | bytes 17367040 | tf_op jit(solution)/shard_map/while/body/eval_jaxpr/dot_general | solution.py:46
  408.3 0.4 dynamic-slice_reduce_fusion.3
  408.7 0.3 and_select_fusion.4
  409.1 0.1 and_select_fusion.5
  409.1 9.2 %fusion.43 = (bf16[256,16384]{1,0:T(8,128)(2,1)}, bf16[256,16384]{1,0:T(8,128)(2,1)}) fusion(s32[16384]{0:T(1024)S(1)} %bitcast.51, bf16[16384]{0:T(1024)(128)(2,1)S(1)} %get-tuple-element.149, bf16[16384]{0:T(1024)(128)(2,1)S(1)} %get-tuple-element.150), kind=kLoop, calls=%fused_computation.6.clone.1 | loop fusion | flops 12582912 | bytes 16908288 | tf_op jit(solution)/shard_map/while/body/eval_jaxpr/jit(_where)/select_n | solution.py:38
  418.3 8.6 %fusion.44 = f32[512,128]{1,0:T(8,128)S(1)} fusion(s32[16384]{0:T(1024)S(1)} %bitcast.55, bf16[256,16384]{1,0:T(8,128)(2,1)} %get-tuple-element.151, bf16[256,16384]{1,0:T(8,128)(2,1)} %get-tuple-element.152, f32[512,128]{1,0:T(8,128)S(1)} %get-tuple-element.161, pred[]{:T(512)S(6)} %compare.24), kind=kOutput, calls=%fused_computation.9.clone.1 | convolution fusion | flops 2183266304 | bytes 17367040 | tf_op jit(solution)/shard_map/while/body/eval_jaxpr/dot_general | solution.py:46
  427.0 0.4 dynamic-slice_reduce_fusion.3
  427.4 0.3 and_select_fusion.4
  427.7 0.1 and_select_fusion.5
  427.8 9.2 %fusion.43 = (bf16[256,16384]{1,0:T(8,128)(2,1)}, bf16[256,16384]{1,0:T(8,128)(2,1)}) fusion(s32[16384]{0:T(1024)S(1)} %bitcast.51, bf16[16384]{0:T(1024)(128)(2,1)S(1)} %get-tuple-element.149, bf16[16384]{0:T(1024)(128)(2,1)S(1)} %get-tuple-element.150), kind=kLoop, calls=%fused_computation.6.clone.1 | loop fusion | flops 12582912 | bytes 16908288 | tf_op jit(solution)/shard_map/while/body/eval_jaxpr/jit(_where)/select_n | solution.py:38
  437.0 8.6 %fusion.44 = f32[512,128]{1,0:T(8,128)S(1)} fusion(s32[16384]{0:T(1024)S(1)} %bitcast.55, bf16[256,16384]{1,0:T(8,128)(2,1)} %get-tuple-element.151, bf16[256,16384]{1,0:T(8,128)(2,1)} %get-tuple-element.152, f32[512,128]{1,0:T(8,128)S(1)} %get-tuple-element.161, pred[]{:T(512)S(6)} %compare.24), kind=kOutput, calls=%fused_computation.9.clone.1 | convolution fusion | flops 2183266304 | bytes 17367040 | tf_op jit(solution)/shard_map/while/body/eval_jaxpr/dot_general | solution.py:46
  445.7 0.7 reshape.57
  446.5 18.2 %reduce-scatter.3.cloned.1.call-done = f32[2,64,128]{2,1,0:T(8,128)} async-done(((f32[2,64,512]{2,1,0:T(8,128)}), f32[2,64,128]{2,1,0:T(8,128)}) %reduce-scatter.3.cloned.1.call-update) | async-done | bytes 65552 | tf_op jit(solution)/shard_map/reduce_scatter | solution.py:94
  464.7 2.1 fusion.14
  466.9 134.0 %reduce-scatter.5.cloned.1.call-done = f32[8,2,128]{2,0,1:T(8,128)} async-done(((f32[512,2,128]{2,0,1:T(8,128)}), f32[8,2,128]{2,0,1:T(8,128)}) %reduce-scatter.5.cloned.1.call-update) | async-done | bytes 8208 | tf_op jit(solution)/shard_map/reduce_scatter | solution.py:99
  600.9 1.3 slice_bitcast_fusion
  (29 shorter events, 0.5 us)
Async XLA Ops:
  7.2 439.3 %copy-start = (s32[64,64]{1,0:T(8,128)S(1)}, s32[64,64]{1,0:T(8,128)}, u32[]{:S(2)}) copy-start(s32[64,64]{1,0:T(8,128)} %param.17) | copy-start | bytes 49156
  7.2 194.4 %all-reduce.2.cloned.1.call-start = ((), (), s32[]{:S(2)}) async-start(), calls=%async_computation.4 | async-start | bytes 2097152 | tf_op jit(solution)/shard_map/psum | solution.py:67
  10.6 266.7 %all-gather.2.cloned.1.call-start = ((), (), s32[]{:S(2)}) async-start(), calls=%async_computation.3 | async-start | bytes 4259840 | tf_op jit(solution)/shard_map/all_gather | solution.py:73
  203.4 112.4 %copy-start.5 = (f32[384]{0:T(512)S(1)}, f32[384]{0:T(512)}, u32[]{:S(2)}) copy-start(f32[384]{0:T(512)} %param.13) | copy-start | bytes 4612
  203.4 112.5 %copy-start.3 = (s32[384]{0:T(512)S(1)}, s32[384]{0:T(512)}, u32[]{:S(2)}) copy-start(s32[384]{0:T(512)} %param.14) | copy-start | bytes 4612
  203.5 112.6 %copy-start.4 = (s32[384]{0:T(512)S(1)}, s32[384]{0:T(512)}, u32[]{:S(2)}) copy-start(s32[384]{0:T(512)} %param.15) | copy-start | bytes 4612
  284.3 32.9 %copy-start.1 = (s32[384,256]{1,0:T(8,128)S(1)}, s32[384,256]{1,0:T(8,128)}, u32[]{:S(2)}) copy-start(s32[384,256]{1,0:T(8,128)} %param.16) | copy-start | bytes 1179652
  302.0 31.6 %copy-start.2 = (f32[64,6]{0,1:T(8,128)}, f32[64,6]{0,1:T(8,128)S(1)}, u32[]{:S(2)}) copy-start(f32[64,6]{0,1:T(8,128)S(1)} %fusion.18) | copy-start | bytes 4612
  307.1 26.2 %all-to-all-start = ((f32[6,64,256]{2,0,1:T(8,128)}), f32[6,64,256]{2,0,1:T(8,128)S(1)}, u32[]{:S(2)}, u32[]{:S(2)}) async-start(f32[6,64,256]{2,0,1:T(8,128)} %bitcast.6), calls=%async_computation | async-start | bytes 1048576 | tf_op jit(solution)/shard_map/all_to_all | solution.py:85
  315.6 149.1 %reduce-scatter.3.cloned.1.call-start = ((), (), s32[]{:S(2)}) async-start(), calls=%async_computation.5 | async-start | bytes 327680 | tf_op jit(solution)/shard_map/reduce_scatter | solution.py:94
  446.5 154.4 %reduce-scatter.5.cloned.1.call-start = ((), (), s32[]{:S(2)}) async-start(), calls=%async_computation.6 | async-start | bytes 532480 | tf_op jit(solution)/shard_map/reduce_scatter | solution.py:99
Sparse Core Ops, SparseCore 0:
  11.4 190.0 all-reduce.1
  204.2 73.0 all-gather.1
  446.6 18.1 reduce-scatter.2
  468.5 132.3 reduce-scatter.4
where the time goes:
time: 609 us
  waiting for transfers between devices  433 us (71%)
  matrix products  76 us (12%)
  other arithmetic  69.9 us (11%)
  between operations  14 us (2%)
  starting transfers between devices  8.88 us (1%)
  local copies, waits for them, and re-layouts  6.68 us (1%)
    psum x1, waiting for transfers between devices, body(): lax.psum(jnp.dot(onehot, timestream, precision=highest, preferred_element...  190 us
    reduce_scatter x1, waiting for transfers between devices, body(): lax.psum_scatter(jnp.einsum('rs,ksp->rkp', selector, shared, precision=hi...  134 us
    all_gather x1, waiting for transfers between devices, body(): all_templates = lax.all_gather(templates, 'span', axis=1, tiled=True)  73.8 us
    select_n x6, other arithmetic, accumulate(): jnp.where(coarse_hot, values_block[None, :], zero_value)  55.2 us
    dot_general x6, matrix products, accumulate(): lax.dot_general(left_hot, right_hot, (((1,), (1,)), ((), ())), preferred_...  51.9 us
    reduce_scatter x1, waiting for transfers between devices, body(): lax.psum_scatter(partial_value, 'wafer', scatter_dimension=2, tiled=True)  18.2 us
    all_to_all x1, waiting for transfers between devices, body(): lax.all_to_all(outgoing, 'span', split_axis=1, concat_axis=0, tiled=True)  16 us
  transfers between devices with their start and end apart: 5, of which 5 were waited for; matrix products, arithmetic and copies ran while one was open for 1% of the time, Pallas kernels for 0%

commit v1 on v0

--- a/solution.py
+++ b/solution.py
@@ -70,7 +70,10 @@
     cleaned = timestream - jnp.dot(
         onehot.T, line_sums * line_scale, precision=highest, preferred_element_type=jnp.float32
     )
-    all_templates = lax.all_gather(templates, "span", axis=1, tiled=True)
+    count = lax.axis_size("span")
+    pieces = jnp.stack([templates for _ in range(count)])
+    pieces = lax.all_to_all(pieces, "span", split_axis=0, concat_axis=0)
+    all_templates = jnp.concatenate(pieces, axis=1)
     normal_matrix = jnp.dot(
         all_templates, all_templates.T, precision=highest, preferred_element_type=jnp.float32
     )

time: 609 us -> 564 us (0.926)
  waiting for transfers between devices: 433 us -> 377 us
  starting transfers between devices: 8.88 us -> 18.5 us
    all_gather x1 -> x0, waiting for transfers between devices: 73.8 us -> none  [body(): all_templates = lax.all_gather(templates, 'span', axis=1, tiled=True)]
    psum x1, waiting for transfers between devices: 190 us -> 209 us  [body(): lax.psum(jnp.dot(onehot, timestream, precision=highest, preferred_element...]
    all_to_all x0 -> x1, starting transfers between devices: none -> 12.2 us  [body(): pieces = lax.all_to_all(pieces, 'span', split_axis=0, concat_axis=0)]
  transfers between devices with their start and end apart: 5 -> 5, of which waited for: 5 -> 4; matrix products, arithmetic and copies ran while one was open for 1% -> 1% of each run, Pallas kernels for 0% -> 0%
where the time goes in v1:
time: 564 us
  waiting for transfers between devices  377 us (67%)
  matrix products  71 us (13%)
  other arithmetic  69.9 us (12%)
  starting transfers between devices  18.5 us (3%)
  between operations  14 us (2%)
  local copies, waits for them, and re-layouts  12.7 us (2%)
    psum x1, waiting for transfers between devices, body(): lax.psum(jnp.dot(onehot, timestream, precision=highest, preferred_element...  209 us
    reduce_scatter x1, waiting for transfers between devices, body(): lax.psum_scatter(jnp.einsum('rs,ksp->rkp', selector, shared, precision=hi...  134 us
    select_n x6, other arithmetic, accumulate(): jnp.where(coarse_hot, values_block[None, :], zero_value)  55.2 us
    dot_general x6, matrix products, accumulate(): lax.dot_general(left_hot, right_hot, (((1,), (1,)), ((), ())), preferred_...  51.9 us
    reduce_scatter x1, waiting for transfers between devices, body(): lax.psum_scatter(partial_value, 'wafer', scatter_dimension=2, tiled=True)  18.2 us
    all_to_all x1, waiting for transfers between devices, body(): lax.all_to_all(outgoing, 'span', split_axis=1, concat_axis=0, tiled=True)  16.1 us
    all_to_all x1, starting transfers between devices, body(): pieces = lax.all_to_all(pieces, 'span', split_axis=0, concat_axis=0)  12.2 us
  transfers between devices with their start and end apart: 5, of which 4 were waited for; matrix products, arithmetic and copies ran while one was open for 1% of the time, Pallas kernels for 0%

profile of v1, /device:TPU:8, one launch (start us, length us, event | category | flops | bytes accessed | tf_op | source)
XLA Modules:
  0.0 563.7 jit_solution(4204769760759083717)
XLA Ops:
  7.2 3.4 stack.2
  10.6 12.2 %all-to-all-start = ((f32[64,64,256]{2,1,0:T(8,128)}), f32[64,64,256]{2,1,0:T(8,128)}, u32[]{:S(2)}, u32[]{:S(2)}) async-start(f32[64,64,256]{2,1,0:T(8,128)} %stack.2), calls=%async_computation | async-start | bytes 8388608 | tf_op jit(solution)/shard_map/all_to_all | solution.py:75
  22.8 0.8 dynamic_slice.27
  23.6 1.5 fusion.28
  25.2 208.8 %all-reduce.2.cloned.1.call-done = f32[12,16384]{1,0:T(8,128)} async-done(((f32[12,16384]{1,0:T(8,128)}), f32[12,16384]{1,0:T(8,128)}) %all-reduce.2.cloned.1.call-update) | async-done | bytes 786448 | tf_op jit(solution)/shard_map/psum | solution.py:67
  233.9 1.7 convolution_subtract_fusion.1
  235.7 6.9 %fusion.13 = f32[64,64]{1,0:T(8,128)S(1)} fusion(f32[64,64,256]{2,1,0:T(8,128)} %all-to-all-done), kind=kOutput, calls=%fused_computation.22 | convolution fusion | flops 805306368 | bytes 4210688 | tf_op jit(solution)/shard_map/dot_general | solution.py:77
  242.7 5.8 %cholesky.16 = f32[64,64]{1,0:T(8,128)S(1)} custom-call(f32[64,64]{1,0:T(8,128)S(1)} %fusion.27), custom_call_target="Cholesky" | custom-call | tf_op jit(solution)/shard_map/jit(cholesky)/cholesky | solution.py:13
  248.6 0.6 compare_reduce_fusion
  249.3 0.7 fusion.22
  249.9 4.9 custom-call.8
  254.9 2.6 copy.16
  257.5 3.3 fusion.32
  260.8 0.3 fusion.25
  261.1 0.2 fusion.23
  261.3 3.1 convolution_subtract_fusion
  264.4 6.2 %all-to-all-start.1 = ((f32[6,64,256]{2,0,1:T(8,128)}), f32[6,64,256]{2,0,1:T(8,128)S(1)}, u32[]{:S(2)}, u32[]{:S(2)}) async-start(f32[6,64,256]{2,0,1:T(8,128)} %bitcast.8), calls=%async_computation.1 | async-start | bytes 1048576 | tf_op jit(solution)/shard_map/all_to_all | solution.py:88
  270.6 0.1 broadcast_in_dim.75
  270.9 0.1 broadcast_bitcast_fusion
  271.0 0.1 copy.20
  271.1 0.1 broadcast_bitcast_fusion.2
  271.2 0.2 copy.18
  271.5 0.1 broadcast_bitcast_fusion.1
  271.6 0.2 copy.19
  271.9 0.1 reshape.66
  272.0 16.1 %all-to-all-done.1 = f32[6,64,256]{2,0,1:T(8,128)S(1)} async-done(((f32[6,64,256]{2,0,1:T(8,128)}), f32[6,64,256]{2,0,1:T(8,128)S(1)}, u32[]{:S(2)}, u32[]{:S(2)}) %all-to-all-start.1) | async-done | bytes 393248 | tf_op jit(solution)/shard_map/all_to_all | solution.py:88
  288.1 0.1 all_to_all.21
  288.3 0.2 multiply_convert_fusion
  288.4 112.1 %while.13 = (s32[]{:T(128)}, f32[512,128]{1,0:T(8,128)S(1)}, s32[6,16384]{1,0:T(8,128)S(1)}, bf16[6,16384]{1,0:T(8,128)(2,1)S(1)}, bf16[6,16384]{1,0:T(8,128)(2,1)S(1)}, /*index=5*/s32[]{:T(128)}, s32[]{:T(128)}) while((s32[]{:T(128)}, f32[512,128]{1,0:T(8,128)S(1)}, s32[6,16384]{1,0:T(8,128)S(1)}, bf16[6,16384]{1,0:T(8,128)(2,1)S(1)}, ...), condition=%wide.region_4.5_spmd.clone, body=%wide.region_3.4_spmd.clone.sunk | while | flops 2196176896 | bytes 34734180 | solution.py:51
  288.5 0.4 dynamic-slice_reduce_fusion.3
  288.9 0.3 and_select_fusion.4
  289.2 0.1 and_select_fusion.5
  289.3 9.2 %fusion.45 = (bf16[256,16384]{1,0:T(8,128)(2,1)}, bf16[256,16384]{1,0:T(8,128)(2,1)}) fusion(s32[16384]{0:T(1024)S(1)} %bitcast.60, bf16[16384]{0:T(1024)(128)(2,1)S(1)} %get-tuple-element.149, bf16[16384]{0:T(1024)(128)(2,1)S(1)} %get-tuple-element.150), kind=kLoop, calls=%fused_computation.6.clone.1 | loop fusion | flops 12582912 | bytes 16908288 | tf_op jit(solution)/shard_map/while/body/eval_jaxpr/jit(_where)/select_n | solution.py:38
  298.5 8.6 %fusion.46 = f32[512,128]{1,0:T(8,128)S(1)} fusion(s32[16384]{0:T(1024)S(1)} %bitcast.64, bf16[256,16384]{1,0:T(8,128)(2,1)} %get-tuple-element.151, bf16[256,16384]{1,0:T(8,128)(2,1)} %get-tuple-element.152, f32[512,128]{1,0:T(8,128)S(1)} %get-tuple-element.161, pred[]{:T(512)S(6)} %compare.24), kind=kOutput, calls=%fused_computation.9.clone.1 | convolution fusion | flops 2183266304 | bytes 17367040 | tf_op jit(solution)/shard_map/while/body/eval_jaxpr/dot_general | solution.py:46
  307.1 0.4 dynamic-slice_reduce_fusion.3
  307.5 0.3 and_select_fusion.4
  307.9 0.1 and_select_fusion.5
  308.0 9.2 %fusion.45 = (bf16[256,16384]{1,0:T(8,128)(2,1)}, bf16[256,16384]{1,0:T(8,128)(2,1)}) fusion(s32[16384]{0:T(1024)S(1)} %bitcast.60, bf16[16384]{0:T(1024)(128)(2,1)S(1)} %get-tuple-element.149, bf16[16384]{0:T(1024)(128)(2,1)S(1)} %get-tuple-element.150), kind=kLoop, calls=%fused_computation.6.clone.1 | loop fusion | flops 12582912 | bytes 16908288 | tf_op jit(solution)/shard_map/while/body/eval_jaxpr/jit(_where)/select_n | solution.py:38
  317.2 8.6 %fusion.46 = f32[512,128]{1,0:T(8,128)S(1)} fusion(s32[16384]{0:T(1024)S(1)} %bitcast.64, bf16[256,16384]{1,0:T(8,128)(2,1)} %get-tuple-element.151, bf16[256,16384]{1,0:T(8,128)(2,1)} %get-tuple-element.152, f32[512,128]{1,0:T(8,128)S(1)} %get-tuple-element.161, pred[]{:T(512)S(6)} %compare.24), kind=kOutput, calls=%fused_computation.9.clone.1 | convolution fusion | flops 2183266304 | bytes 17367040 | tf_op jit(solution)/shard_map/while/body/eval_jaxpr/dot_general | solution.py:46
  325.8 0.4 dynamic-slice_reduce_fusion.3
  326.2 0.3 and_select_fusion.4
  326.6 0.1 and_select_fusion.5
  326.7 9.2 %fusion.45 = (bf16[256,16384]{1,0:T(8,128)(2,1)}, bf16[256,16384]{1,0:T(8,128)(2,1)}) fusion(s32[16384]{0:T(1024)S(1)} %bitcast.60, bf16[16384]{0:T(1024)(128)(2,1)S(1)} %get-tuple-element.149, bf16[16384]{0:T(1024)(128)(2,1)S(1)} %get-tuple-element.150), kind=kLoop, calls=%fused_computation.6.clone.1 | loop fusion | flops 12582912 | bytes 16908288 | tf_op jit(solution)/shard_map/while/body/eval_jaxpr/jit(_where)/select_n | solution.py:38
  335.9 8.6 %fusion.46 = f32[512,128]{1,0:T(8,128)S(1)} fusion(s32[16384]{0:T(1024)S(1)} %bitcast.64, bf16[256,16384]{1,0:T(8,128)(2,1)} %get-tuple-element.151, bf16[256,16384]{1,0:T(8,128)(2,1)} %get-tuple-element.152, f32[512,128]{1,0:T(8,128)S(1)} %get-tuple-element.161, pred[]{:T(512)S(6)} %compare.24), kind=kOutput, calls=%fused_computation.9.clone.1 | convolution fusion | flops 2183266304 | bytes 17367040 | tf_op jit(solution)/shard_map/while/body/eval_jaxpr/dot_general | solution.py:46
  344.5 0.4 dynamic-slice_reduce_fusion.3
  344.9 0.3 and_select_fusion.4
  345.3 0.1 and_select_fusion.5
  345.4 9.2 %fusion.45 = (bf16[256,16384]{1,0:T(8,128)(2,1)}, bf16[256,16384]{1,0:T(8,128)(2,1)}) fusion(s32[16384]{0:T(1024)S(1)} %bitcast.60, bf16[16384]{0:T(1024)(128)(2,1)S(1)} %get-tuple-element.149, bf16[16384]{0:T(1024)(128)(2,1)S(1)} %get-tuple-element.150), kind=kLoop, calls=%fused_computation.6.clone.1 | loop fusion | flops 12582912 | bytes 16908288 | tf_op jit(solution)/shard_map/while/body/eval_jaxpr/jit(_where)/select_n | solution.py:38
  354.6 8.6 %fusion.46 = f32[512,128]{1,0:T(8,128)S(1)} fusion(s32[16384]{0:T(1024)S(1)} %bitcast.64, bf16[256,16384]{1,0:T(8,128)(2,1)} %get-tuple-element.151, bf16[256,16384]{1,0:T(8,128)(2,1)} %get-tuple-element.152, f32[512,128]{1,0:T(8,128)S(1)} %get-tuple-element.161, pred[]{:T(512)S(6)} %compare.24), kind=kOutput, calls=%fused_computation.9.clone.1 | convolution fusion | flops 2183266304 | bytes 17367040 | tf_op jit(solution)/shard_map/while/body/eval_jaxpr/dot_general | solution.py:46
  363.2 0.4 dynamic-slice_reduce_fusion.3
  363.6 0.3 and_select_fusion.4
  364.0 0.1 and_select_fusion.5
  364.0 9.2 %fusion.45 = (bf16[256,16384]{1,0:T(8,128)(2,1)}, bf16[256,16384]{1,0:T(8,128)(2,1)}) fusion(s32[16384]{0:T(1024)S(1)} %bitcast.60, bf16[16384]{0:T(1024)(128)(2,1)S(1)} %get-tuple-element.149, bf16[16384]{0:T(1024)(128)(2,1)S(1)} %get-tuple-element.150), kind=kLoop, calls=%fused_computation.6.clone.1 | loop fusion | flops 12582912 | bytes 16908288 | tf_op jit(solution)/shard_map/while/body/eval_jaxpr/jit(_where)/select_n | solution.py:38
  373.2 8.6 %fusion.46 = f32[512,128]{1,0:T(8,128)S(1)} fusion(s32[16384]{0:T(1024)S(1)} %bitcast.64, bf16[256,16384]{1,0:T(8,128)(2,1)} %get-tuple-element.151, bf16[256,16384]{1,0:T(8,128)(2,1)} %get-tuple-element.152, f32[512,128]{1,0:T(8,128)S(1)} %get-tuple-element.161, pred[]{:T(512)S(6)} %compare.24), kind=kOutput, calls=%fused_computation.9.clone.1 | convolution fusion | flops 2183266304 | bytes 17367040 | tf_op jit(solution)/shard_map/while/body/eval_jaxpr/dot_general | solution.py:46
  381.9 0.4 dynamic-slice_reduce_fusion.3
  382.3 0.3 and_select_fusion.4
  382.6 0.1 and_select_fusion.5
  382.7 9.2 %fusion.45 = (bf16[256,16384]{1,0:T(8,128)(2,1)}, bf16[256,16384]{1,0:T(8,128)(2,1)}) fusion(s32[16384]{0:T(1024)S(1)} %bitcast.60, bf16[16384]{0:T(1024)(128)(2,1)S(1)} %get-tuple-element.149, bf16[16384]{0:T(1024)(128)(2,1)S(1)} %get-tuple-element.150), kind=kLoop, calls=%fused_computation.6.clone.1 | loop fusion | flops 12582912 | bytes 16908288 | tf_op jit(solution)/shard_map/while/body/eval_jaxpr/jit(_where)/select_n | solution.py:38
  391.9 8.6 %fusion.46 = f32[512,128]{1,0:T(8,128)S(1)} fusion(s32[16384]{0:T(1024)S(1)} %bitcast.64, bf16[256,16384]{1,0:T(8,128)(2,1)} %get-tuple-element.151, bf16[256,16384]{1,0:T(8,128)(2,1)} %get-tuple-element.152, f32[512,128]{1,0:T(8,128)S(1)} %get-tuple-element.161, pred[]{:T(512)S(6)} %compare.24), kind=kOutput, calls=%fused_computation.9.clone.1 | convolution fusion | flops 2183266304 | bytes 17367040 | tf_op jit(solution)/shard_map/while/body/eval_jaxpr/dot_general | solution.py:46
  400.6 0.7 reshape.67
  401.4 18.2 %reduce-scatter.3.cloned.1.call-done = f32[2,64,128]{2,1,0:T(8,128)} async-done(((f32[2,64,512]{2,1,0:T(8,128)}), f32[2,64,128]{2,1,0:T(8,128)}) %reduce-scatter.3.cloned.1.call-update) | async-done | bytes 65552 | tf_op jit(solution)/shard_map/reduce_scatter | solution.py:97
  419.7 2.1 fusion.19
  421.8 134.1 %reduce-scatter.5.cloned.1.call-done = f32[8,2,128]{2,0,1:T(8,128)} async-done(((f32[512,2,128]{2,0,1:T(8,128)}), f32[8,2,128]{2,0,1:T(8,128)}) %reduce-scatter.5.cloned.1.call-update) | async-done | bytes 8208 | tf_op jit(solution)/shard_map/reduce_scatter | solution.py:102
  555.9 1.3 slice_bitcast_fusion
  (32 shorter events, 0.6 us)
Async XLA Ops:
  7.2 394.2 %copy-start = (s32[64,64]{1,0:T(8,128)S(1)}, s32[64,64]{1,0:T(8,128)}, u32[]{:S(2)}) copy-start(s32[64,64]{1,0:T(8,128)} %param.17) | copy-start | bytes 49156
  7.2 16.4 %copy-start.1 = (f32[6,16384]{1,0:T(8,128)S(1)}, f32[6,16384]{1,0:T(8,128)}, u32[]{:S(2)}) copy-start(f32[6,16384]{1,0:T(8,128)} %param.10) | copy-start | bytes 1179652
  10.6 225.1 %all-to-all-start = ((f32[64,64,256]{2,1,0:T(8,128)}), f32[64,64,256]{2,1,0:T(8,128)}, u32[]{:S(2)}, u32[]{:S(2)}) async-start(f32[64,64,256]{2,1,0:T(8,128)} %stack.2), calls=%async_computation | async-start | bytes 8388608 | tf_op jit(solution)/shard_map/all_to_all | solution.py:75
  22.8 211.2 %all-reduce.2.cloned.1.call-start = ((), (), s32[]{:S(2)}) async-start(), calls=%async_computation.4 | async-start | bytes 2097152 | tf_op jit(solution)/shard_map/psum | solution.py:67
  254.8 15.8 %copy-start.6 = (f32[384]{0:T(512)S(1)}, f32[384]{0:T(512)}, u32[]{:S(2)}) copy-start(f32[384]{0:T(512)} %param.13) | copy-start | bytes 4612
  254.8 15.8 %copy-start.4 = (s32[384]{0:T(512)S(1)}, s32[384]{0:T(512)}, u32[]{:S(2)}) copy-start(s32[384]{0:T(512)} %param.14) | copy-start | bytes 4612
  254.9 15.9 %copy-start.5 = (s32[384]{0:T(512)S(1)}, s32[384]{0:T(512)}, u32[]{:S(2)}) copy-start(s32[384]{0:T(512)} %param.15) | copy-start | bytes 4612
  257.5 14.4 %copy-start.2 = (s32[384,256]{1,0:T(8,128)S(1)}, s32[384,256]{1,0:T(8,128)}, u32[]{:S(2)}) copy-start(s32[384,256]{1,0:T(8,128)} %param.16) | copy-start | bytes 1179652
  261.3 27.1 %copy-start.3 = (f32[64,6]{0,1:T(8,128)}, f32[64,6]{0,1:T(8,128)S(1)}, u32[]{:S(2)}) copy-start(f32[64,6]{0,1:T(8,128)S(1)} %fusion.23) | copy-start | bytes 4612
  264.4 23.8 %all-to-all-start.1 = ((f32[6,64,256]{2,0,1:T(8,128)}), f32[6,64,256]{2,0,1:T(8,128)S(1)}, u32[]{:S(2)}, u32[]{:S(2)}) async-start(f32[6,64,256]{2,0,1:T(8,128)} %bitcast.8), calls=%async_computation.1 | async-start | bytes 1048576 | tf_op jit(solution)/shard_map/all_to_all | solution.py:88
  270.5 149.1 %reduce-scatter.3.cloned.1.call-start = ((), (), s32[]{:S(2)}) async-start(), calls=%async_computation.5 | async-start | bytes 327680 | tf_op jit(solution)/shard_map/reduce_scatter | solution.py:97
  401.4 154.6 %reduce-scatter.5.cloned.1.call-start = ((), (), s32[]{:S(2)}) async-start(), calls=%async_computation.6 | async-start | bytes 532480 | tf_op jit(solution)/shard_map/reduce_scatter | solution.py:102
Sparse Core Ops, SparseCore 0:
  27.0 206.8 all-reduce.1
  401.5 18.1 reduce-scatter.2
  423.5 132.3 reduce-scatter.4
